TPU v7x, 32 devices: a whole 2x2x4 slice. The times are simulated.
32 devices in a mesh: dp: 8 (over y, x, core), chan: 4 (over z).
Axes of the slice: x: 2, y: 2, z: 4, core: 2. Of those that a mesh axis runs over, the one named last changes fastest.
Arguments:
- signal: bfloat16 [8, 512, 8192], P('dp', 'chan'), may hold values from -6 to 6
- signal_grad: bfloat16 [8, 512, 8192], P('dp', 'chan'), may hold values from -6 to 6
- embed_weight: float32 [64, 33], replicated, may hold values from -1 to 1
- embed_bias: float32 [64], replicated, may hold values from -3.140625 to 3.140625
- hidden_weight: float32 [64, 64], replicated, may hold values from -0.75 to 0.75
- frequency: float32 [2, 64], replicated, may hold values from 0.5 to 2
- output_weight: float32 [512, 64], replicated, may hold values from -0.75 to 0.75
- decay_rate: float32 [512], replicated, may hold values from 0.3 to 30
Outputs:
- filter_grad: float32 [512, 16384], P(None, ('dp', 'chan'))
- embed_grad: float32 [64, 33], replicated
- bias_grad: float32 [64], replicated
- hidden_grad: float32 [64, 64], replicated
- frequency_grad: float32 [2, 64], replicated
- output_grad: float32 [512, 64], replicated
- decay_grad: float32 [512], replicated
All inputs are finite; a program needn't handle non-finite values.
Results may differ from a plain program's by a relative error of at most 0.0003.
Values may be sent and summed in bfloat16 or wider, within the bound.
No kernel may reach another device: no remote copies, remote signals or barrier semaphores. Data moves between devices by JAX's collectives and lax.ppermute only.
A program may use at most 64 MiB of HBM per device.

v0:
```python
import math
import jax
import jax.numpy as jnp
from jax import lax
from jax.sharding import PartitionSpec as P


def lag_features(lag, length, bands):
    total = 2 * length
    scaled = lag.astype(jnp.float32) / length
    sines = []
    cosines = []
    for band in range(bands):
        factor = max(1, int(0.45 * total * 10000.0 ** (-band / bands)))
        phase = (lag * factor % total).astype(jnp.float32) * (2.0 * math.pi / total)
        sines.append(jnp.sin(phase))
        cosines.append(jnp.cos(phase))
    return jnp.stack([scaled] + sines + cosines)


def filter_loss(params, lag, cotangent, length):
    embed_weight, embed_bias, hidden_weight, frequency, output_weight, decay_rate = params
    bands = (embed_weight.shape[1] - 1) // 2
    exact = lax.Precision.HIGHEST
    table = lag_features(lag, length, bands)
    first = jnp.sin(
        frequency[0][:, None]
        * (
            jnp.dot(embed_weight, table, precision=exact, preferred_element_type=jnp.float32)
            + embed_bias[:, None]
        )
    )
    second = jnp.sin(
        frequency[1][:, None]
        * jnp.dot(hidden_weight, first, precision=exact, preferred_element_type=jnp.float32)
    )
    shaped = jnp.dot(output_weight, second, precision=exact, preferred_element_type=jnp.float32)
    window = jnp.exp(-decay_rate[:, None] * jnp.abs(lag).astype(jnp.float32)[None, :] / length)
    return jnp.sum(shaped * window * cotangent) / math.sqrt(2 * length)


def plan_sizes(total):
    bits = total.bit_length() - 1
    side = 2 ** min(7, bits // 2)
    return (total // (side * side), side, side)


def rotation(rows, cols, modulus, sign):
    row_index = jnp.arange(rows, dtype=jnp.int32)
    col_index = jnp.arange(cols, dtype=jnp.int32)
    product = row_index[:, None] * col_index[None, :] % modulus
    angle = product.astype(jnp.float32) * (-2.0 * math.pi / modulus)
    return (jnp.cos(angle), sign * jnp.sin(angle))


def twist(real_part, imag_part, table):
    cosine, sine = table
    return (real_part * cosine - imag_part * sine, real_part * sine + imag_part * cosine)


def table_product(spec, table, real_part, imag_part, table_first):
    cosine, sine = table
    exact = lax.Precision.HIGHEST

    def apply(matrix, values):
        if table_first:
            return jnp.einsum(
                spec, matrix, values, precision=exact, preferred_element_type=jnp.float32
            )
        return jnp.einsum(spec, values, matrix, precision=exact, preferred_element_type=jnp.float32)

    common = apply(cosine, real_part + imag_part)
    return (common - apply(cosine + sine, imag_part), common + apply(sine - cosine, real_part))


def forward(real_part, imag_part, total):
    outer, middle, inner = plan_sizes(total)
    leading = real_part.shape[:-1]
    real_part = real_part.reshape(leading + (outer, middle * inner))
    imag_part = imag_part.reshape(leading + (outer, middle * inner))
    real_part, imag_part = table_product(
        "kp,...pm->...km", rotation(outer, outer, outer, 1.0), real_part, imag_part, True
    )
    real_part, imag_part = twist(real_part, imag_part, rotation(outer, middle * inner, total, 1.0))
    real_part = real_part.reshape(leading + (outer, middle, inner))
    imag_part = imag_part.reshape(leading + (outer, middle, inner))
    real_part, imag_part = table_product(
        "aq,...kqr->...kar", rotation(middle, middle, middle, 1.0), real_part, imag_part, True
    )
    real_part, imag_part = twist(real_part, imag_part, rotation(middle, inner, middle * inner, 1.0))
    return table_product(
        "...kar,rb->...kab", rotation(inner, inner, inner, 1.0), real_part, imag_part, False
    )


def inverse(real_part, imag_part, total):
    outer, middle, inner = plan_sizes(total)
    leading = real_part.shape[:-3]
    exact = lax.Precision.HIGHEST
    real_part, imag_part = table_product(
        "...kab,rb->...kar", rotation(inner, inner, inner, -1.0), real_part, imag_part, False
    )
    real_part, imag_part = twist(
        real_part, imag_part, rotation(middle, inner, middle * inner, -1.0)
    )
    real_part, imag_part = table_product(
        "qa,...kar->...kqr", rotation(middle, middle, middle, -1.0), real_part, imag_part, True
    )
    real_part = real_part.reshape(leading + (outer, middle * inner))
    imag_part = imag_part.reshape(leading + (outer, middle * inner))
    real_part, imag_part = twist(real_part, imag_part, rotation(outer, middle * inner, total, -1.0))
    cosine, sine = rotation(outer, outer, outer, -1.0)
    result = jnp.einsum(
        "pk,...km->...pm", cosine, real_part, precision=exact, preferred_element_type=jnp.float32
    )
    result = result - jnp.einsum(
        "pk,...km->...pm", sine, imag_part, precision=exact, preferred_element_type=jnp.float32
    )
    return result.reshape(leading + (total,)) / total


def mirror(values):
    flipped = jnp.flip(values, (-3, -2, -1))
    shifted = jnp.roll(flipped, 1, axis=-3)
    head = jnp.roll(shifted[..., 0, :, :], 1, axis=-2)
    first_row = (jnp.arange(head.shape[-2]) == 0)[:, None]
    head = jnp.where(first_row, jnp.roll(head, 1, axis=-1), head)
    return jnp.concatenate([head[..., None, :, :], shifted[..., 1:, :, :]], axis=-3)


def block_spectrum(inputs, grads, total):
    padding = jnp.zeros(inputs.shape[:-1] + (total - inputs.shape[-1],), jnp.float32)
    real_part = jnp.concatenate([inputs.astype(jnp.float32), padding], axis=-1)
    imag_part = jnp.concatenate([grads.astype(jnp.float32), padding], axis=-1)
    spectrum_real, spectrum_imag = forward(real_part, imag_part, total)
    back_real = mirror(spectrum_real)
    back_imag = -mirror(spectrum_imag)
    in_real = 0.5 * (spectrum_real + back_real)
    in_imag = 0.5 * (spectrum_imag + back_imag)
    grad_real = 0.5 * (spectrum_imag - back_imag)
    grad_imag = -0.5 * (spectrum_real - back_real)
    cross_real = in_real * grad_real + in_imag * grad_imag
    cross_imag = in_real * grad_imag - in_imag * grad_real
    return (jnp.sum(cross_real, axis=0), jnp.sum(cross_imag, axis=0))


def local(
    signal,
    signal_grad,
    embed_weight,
    embed_bias,
    hidden_weight,
    frequency,
    output_weight,
    decay_rate,
):
    seq_local, chan_local, length = signal.shape
    total = 2 * length
    block = 8
    scale = 1.0 / math.sqrt(seq_local * lax.axis_size("dp") * length)
    indices = jnp.arange(chan_local // block, dtype=jnp.int32)

    def spectrum_of(index):
        start = index * block
        inputs = lax.dynamic_slice_in_dim(signal, start, block, 1)
        grads = lax.dynamic_slice_in_dim(signal_grad, start, block, 1)
        return block_spectrum(inputs, grads, total)

    def lags_of(index):
        cross_real, cross_imag = spectrum_of(index)
        return inverse(cross_real, cross_imag, total)

    correlation = lax.map(lags_of, indices).reshape(chan_local, total) * scale
    shared = lax.psum_scatter(correlation, "dp", scatter_dimension=1, tiled=True)
    filter_grad = lax.all_to_all(shared, "chan", split_axis=1, concat_axis=0, tiled=True)
    lag_count = filter_grad.shape[1]
    device_rank = lax.axis_index("dp") * lax.axis_size("chan") + lax.axis_index("chan")
    position = device_rank * lag_count + jnp.arange(lag_count, dtype=jnp.int32)
    lag = jnp.where(position < length, position, position - total)
    params = (embed_weight, embed_bias, hidden_weight, frequency, output_weight, decay_rate)
    local_grads = jax.grad(filter_loss)(params, lag, filter_grad, length)
    summed = lax.psum(
        (
            local_grads[0],
            local_grads[1],
            local_grads[2],
            local_grads[3],
            local_grads[4],
            local_grads[5],
        ),
        ("dp", "chan"),
    )
    return (filter_grad, summed[0], summed[1], summed[2], summed[3], summed[4], summed[5])


def solution(mesh):
    placed = (P("dp", "chan", None), P("dp", "chan", None), P(), P(), P(), P(), P(), P())
    return jax.shard_map(
        local,
        mesh=mesh,
        in_specs=placed,
        out_specs=(P(None, ("dp", "chan")), P(), P(), P(), P(), P(), P()),
        check_vma=False,
    )
```

profile of v0, /device:TPU:0, one launch (start us, length us, event | category | flops | bytes accessed | tf_op | source)
XLA Modules:
  0.0 587.0 jit_solution(18230572061578156664)
XLA Ops:
  7.2 325.0 %while.13 = (s32[]{:T(128)}, f32[16,8,16384]{2,1,0:T(8,128)}, s32[16]{0:T(128)S(1)}, bf16[1,128,8192]{2,1,0:T(8,128)(2,1)}, bf16[1,128,8192]{2,1,0:T(8,128)(2,1)...) while((s32[]{:T(128)}, f32[16,8,16384]{2,1,0:T(8,128)}, s32[16]{0:T(128)S(1)}, ...), condition=%wide.region_1.2_spmd, body=%wide.region_0.1_spmd.sunk | while | flops 2430353408 | bytes 44499364 | solution.py:173
  13.4 1.3 fusion.309
  22.5 1.3 fusion.317
  25.0 1.2 subtract_multiply_fusion.4
  33.7 1.3 fusion.309
  42.9 1.3 fusion.317
  45.4 1.2 subtract_multiply_fusion.4
  54.0 1.3 fusion.309
  63.2 1.3 fusion.317
  65.7 1.2 subtract_multiply_fusion.4
  74.4 1.3 fusion.309
  83.5 1.3 fusion.317
  94.7 1.3 fusion.309
  103.8 1.3 fusion.317
  115.0 1.3 fusion.309
  124.2 1.3 fusion.317
  135.3 1.3 fusion.309
  144.5 1.3 fusion.317
  155.6 1.3 fusion.309
  164.8 1.3 fusion.317
  175.9 1.3 fusion.309
  185.1 1.3 fusion.317
  196.3 1.3 fusion.309
  205.4 1.3 fusion.317
  216.6 1.3 fusion.309
  225.7 1.3 fusion.317
  236.9 1.3 fusion.309
  246.0 1.3 fusion.317
  257.2 1.3 fusion.309
  266.4 1.3 fusion.317
  277.5 1.3 fusion.309
  286.7 1.3 fusion.317
  297.8 1.3 fusion.309
  307.0 1.3 fusion.317
  318.1 1.3 fusion.309
  327.3 1.3 fusion.317
  332.3 7.4 %multiply_bitcast_fusion = f32[128,16384]{1,0:T(8,128)} fusion(f32[16,8,16384]{2,1,0:T(8,128)} %get-tuple-element.175), kind=kLoop, calls=%fused_computation.149 | loop fusion | flops 2097152 | bytes 16777216 | tf_op jit(solution)/shard_map/mul | solution.py:173
  342.0 72.2 %reduce-scatter.2.cloned.1.call-done = f32[128,2048]{1,0:T(8,128)} async-done(((f32[128,16384]{1,0:T(8,128)}), f32[128,2048]{1,0:T(8,128)}) %reduce-scatter.2.cloned.1.call-update) | async-done | bytes 1048592 | tf_op jit(solution)/shard_map/reduce_scatter | solution.py:174
  414.1 2.5 copy.73
  416.7 4.6 all-to-all-start
  423.4 23.4 %all-to-all-done = f32[128,4,512]{0,2,1:T(8,128)S(1)} async-done(((f32[128,4,512]{0,2,1:T(8,128)}), f32[128,4,512]{0,2,1:T(8,128)S(1)}, u32[]{:S(2)}, u32[]{:S(2)}) %all-to-all-start) | async-done | bytes 1048608 | tf_op jit(solution)/shard_map/all_to_all | solution.py:175
  446.8 1.8 multiply_reduce_fusion.1
  450.4 1.3 copy.75
  452.0 1.7 fusion.113
  453.7 2.2 fusion.118
  455.9 38.1 %all-reduce.4 = (f32[64,33]{0,1:T(8,128)}, f32[64]{0:T(128)}, f32[64,64]{1,0:T(8,128)}, f32[2,64]{1,0:T(2,128)}, f32[512]{0:T(512)}) all-reduce(f32[64,33]{0,1:T(8,128)S(1)} %fusion.129, f32[64]{0:T(128)S(1)} %get-tuple-element.198, f32[64,64]{1,0:T(8,128)S(1)} %fusion.131, ...), channel_id=1, replica_groups=mesh['dp'=8,'chan'=4] {'dp','chan'}, use_global_device_ids=true, to_apply=%region_3.4 | all-reduce | flops 6912 | bytes 55296 | tf_op jit(solution)/shard_map/psum | solution.py:182
  494.0 84.7 %all-reduce.7.cloned.1.call-done = f32[512,64]{0,1:T(8,128)} async-done(((f32[512,64]{0,1:T(8,128)}), f32[512,64]{0,1:T(8,128)}) %all-reduce.7.cloned.1.call-update) | async-done | bytes 131088 | tf_op jit(solution)/shard_map/psum | solution.py:182
  578.6 1.6 copy.124
  (589 shorter events, 273.2 us)
Async XLA Ops:
  7.2 439.7 %copy-start = (f32[512,64]{0,1:T(8,128)S(1)}, f32[512,64]{0,1:T(8,128)}, u32[]{:S(2)}) copy-start(f32[512,64]{0,1:T(8,128)} %param.16) | copy-start | bytes 393220
  7.2 407.0 %reduce-scatter.2.cloned.1.call-start = ((), (), s32[]{:S(2)}) async-start(), calls=%async_computation.2 | async-start | bytes 9437184 | tf_op jit(solution)/shard_map/reduce_scatter | solution.py:174
  339.7 0.7 copy-start.3
  339.7 82.6 %copy-start.4 = (f32[2,64]{1,0:T(2,128)S(1)}, f32[2,64]{1,0:T(2,128)}, u32[]{:S(2)}) copy-start(f32[2,64]{1,0:T(2,128)} %param.15) | copy-start | bytes 1540
  339.7 82.6 %copy-start.2 = (f32[64,33]{0,1:T(8,128)S(1)}, f32[64,33]{0,1:T(8,128)}, u32[]{:S(2)}) copy-start(f32[64,33]{0,1:T(8,128)} %param.12) | copy-start | bytes 25348
  339.7 82.6 %copy-start.5 = (f32[64]{0:T(128)S(1)}, f32[64]{0:T(128)}, u32[]{:S(2)}) copy-start(f32[64]{0:T(128)} %param.13) | copy-start | bytes 772
  339.7 82.9 %copy-start.1 = (f32[64,64]{1,0:T(8,128)S(1)}, f32[64,64]{1,0:T(8,128)}, u32[]{:S(2)}) copy-start(f32[64,64]{1,0:T(8,128)} %param.14) | copy-start | bytes 49156
  416.7 30.2 %all-to-all-start = ((f32[128,4,512]{0,2,1:T(8,128)}), f32[128,4,512]{0,2,1:T(8,128)S(1)}, u32[]{:S(2)}, u32[]{:S(2)}) async-start(f32[128,4,512]{0,2,1:T(8,128)} %bitcast.39), calls=%async_computation.1 | async-start | bytes 2097152 | tf_op jit(solution)/shard_map/all_to_all | solution.py:175
  421.3 157.4 %all-reduce.7.cloned.1.call-start = ((), (), s32[]{:S(2)}) async-start(), calls=%async_computation.3 | async-start | bytes 262144 | tf_op jit(solution)/shard_map/psum | solution.py:182
Sparse Core Ops, SparseCore 0:
  339.9 74.2 reduce-scatter.1
  456.0 122.5 all-reduce.6
where the time goes:
time: 588 us; the launch traced here: 587 us
  matrix products  207 us (35%)
  waiting for transfers between devices  180 us (31%)
  local copies, waits for them, and re-layouts  88.7 us (15%)
  other arithmetic  40.2 us (7%)
  blocking collectives  38.1 us (6%)
  between operations  14.2 us (2%)
  loops' own time  14 us (2%)
    dot_general x96, matrix products, apply(): jnp.einsum(spec, values, matrix, precision=exact, preferred_element_type=...  99.2 us
    dot_general x96, matrix products, apply(): jnp.einsum(spec, matrix, values, precision=exact, preferred_element_type=...  99.1 us
    psum x1, waiting for transfers between devices, local(): lax.psum((local_grads[0], local_grads[1], local_grads[2], local_grads[3],...  84.7 us
    reduce_scatter x1, waiting for transfers between devices, local(): lax.psum_scatter(correlation, 'dp', scatter_dimension=1, tiled=True)  72.2 us
    psum x1, blocking collectives, local(): lax.psum((local_grads[0], local_grads[1], local_grads[2], local_grads[3],...  38.1 us
    all_to_all x1, waiting for transfers between devices, local(): lax.all_to_all(shared, 'chan', split_axis=1, concat_axis=0, tiled=True)  23.4 us
    another operation x32, local copies, waits for them, and re-layouts  22.9 us
    dynamic_update_slice x16, local copies, waits for them, and re-layouts, local(): correlation = lax.map(lags_of, indices).reshape(chan_local, total) * scale  18 us
  transfers between devices with their start and end apart: 3, of which 3 were waited for; matrix products, arithmetic and copies ran while one was open for 1% of the time, Pallas kernels for 0%

commit v1 on v0

--- a/solution.py
+++ b/solution.py
@@ -180,15 +180,18 @@
     params = (embed_weight, embed_bias, hidden_weight, frequency, output_weight, decay_rate)
     local_grads = jax.grad(filter_loss)(params, lag, filter_grad, length)
     summed = lax.psum(
-        (
-            local_grads[0],
-            local_grads[1],
-            local_grads[2],
-            local_grads[3],
-            local_grads[4],
-            local_grads[5],
+        lax.psum(
+            (
+                local_grads[0],
+                local_grads[1],
+                local_grads[2],
+                local_grads[3],
+                local_grads[4],
+                local_grads[5],
+            ),
+            "chan",
         ),
-        ("dp", "chan"),
+        "dp",
     )
     return (filter_grad, summed[0], summed[1], summed[2], summed[3], summed[4], summed[5])
 

time: 588 us -> 551 us (0.937)
  waiting for transfers between devices: 180 us -> 140 us
    psum x1, waiting for transfers between devices: 84.7 us -> 31 us  [local(): lax.psum((local_grads[0], local_grads[1], local_grads[2], local_grads[3],...]
    psum x0 -> x1, blocking collectives: none -> 23.4 us  [local(): lax.psum(lax.psum((local_grads[0], local_grads[1], local_grads[2], local_...]
    psum x1, blocking collectives: 38.1 us -> 18.4 us  [local(): lax.psum((local_grads[0], local_grads[1], local_grads[2], local_grads[3],...]
    psum x0 -> x1, waiting for transfers between devices: none -> 13 us  [local(): lax.psum(lax.psum((local_grads[0], local_grads[1], local_grads[2], local_...]
  transfers between devices with their start and end apart: 3 -> 4, of which waited for: 3 -> 4; matrix products, arithmetic and copies ran while one was open for 1% -> 1% of each run, Pallas kernels for 0% -> 0%
where the time goes in v1:
time: 551 us; the launch traced here: 550 us
  matrix products  207 us (38%)
  waiting for transfers between devices  140 us (25%)
  local copies, waits for them, and re-layouts  88.7 us (16%)
  blocking collectives  41.8 us (8%)
  other arithmetic  40.2 us (7%)
  loops' own time  14 us (3%)
  between operations  13.9 us (3%)
    dot_general x96, matrix products, apply(): jnp.einsum(spec, values, matrix, precision=exact, preferred_element_type=...  99.2 us
    dot_general x96, matrix products, apply(): jnp.einsum(spec, matrix, values, precision=exact, preferred_element_type=...  99.1 us
    reduce_scatter x1, waiting for transfers between devices, local(): lax.psum_scatter(correlation, 'dp', scatter_dimension=1, tiled=True)  72.2 us
    psum x1, waiting for transfers between devices, local(): lax.psum((local_grads[0], local_grads[1], local_grads[2], local_grads[3],...  31 us
    all_to_all x1, waiting for transfers between devices, local(): lax.all_to_all(shared, 'chan', split_axis=1, concat_axis=0, tiled=True)  23.4 us
    psum x1, blocking collectives, local(): lax.psum(lax.psum((local_grads[0], local_grads[1], local_grads[2], local_...  23.4 us
    another operation x32, local copies, waits for them, and re-layouts  22.9 us
    psum x1, blocking collectives, local(): lax.psum((local_grads[0], local_grads[1], local_grads[2], local_grads[3],...  18.4 us
  transfers between devices with their start and end apart: 4, of which 4 were waited for; matrix products, arithmetic and copies ran while one was open for 1% of the time, Pallas kernels for 0%

profile of v1, /device:TPU:0, one launch (start us, length us, event | category | flops | bytes accessed | tf_op | source)
XLA Modules:
  0.0 549.9 jit_solution(15306935509039255713)
XLA Ops:
  7.2 325.0 %while.13 = (s32[]{:T(128)}, f32[16,8,16384]{2,1,0:T(8,128)}, s32[16]{0:T(128)S(1)}, bf16[1,128,8192]{2,1,0:T(8,128)(2,1)}, bf16[1,128,8192]{2,1,0:T(8,128)(2,1)...) while((s32[]{:T(128)}, f32[16,8,16384]{2,1,0:T(8,128)}, s32[16]{0:T(128)S(1)}, ...), condition=%wide.region_1.2_spmd, body=%wide.region_0.1_spmd.sunk | while | flops 2430353408 | bytes 44499364 | solution.py:173
  13.4 1.3 fusion.309
  22.5 1.3 fusion.317
  25.0 1.2 subtract_multiply_fusion.4
  33.7 1.3 fusion.309
  42.9 1.3 fusion.317
  54.0 1.3 fusion.309
  63.2 1.3 fusion.317
  74.3 1.3 fusion.309
  83.5 1.3 fusion.317
  94.7 1.3 fusion.309
  103.8 1.3 fusion.317
  115.0 1.3 fusion.309
  124.1 1.3 fusion.317
  135.3 1.3 fusion.309
  144.4 1.3 fusion.317
  155.5 1.3 fusion.309
  164.7 1.3 fusion.317
  175.9 1.3 fusion.309
  185.0 1.3 fusion.317
  196.2 1.3 fusion.309
  205.4 1.3 fusion.317
  216.5 1.3 fusion.309
  225.7 1.3 fusion.317
  236.8 1.3 fusion.309
  246.0 1.3 fusion.317
  257.2 1.3 fusion.309
  266.3 1.3 fusion.317
  277.5 1.3 fusion.309
  286.6 1.3 fusion.317
  297.8 1.3 fusion.309
  306.9 1.3 fusion.317
  318.1 1.3 fusion.309
  327.2 1.3 fusion.317
  332.3 7.4 %multiply_bitcast_fusion = f32[128,16384]{1,0:T(8,128)} fusion(f32[16,8,16384]{2,1,0:T(8,128)} %get-tuple-element.175), kind=kLoop, calls=%fused_computation.149 | loop fusion | flops 2097152 | bytes 16777216 | tf_op jit(solution)/shard_map/mul | solution.py:173
  341.9 72.2 %reduce-scatter.2.cloned.1.call-done = f32[128,2048]{1,0:T(8,128)} async-done(((f32[128,16384]{1,0:T(8,128)}), f32[128,2048]{1,0:T(8,128)}) %reduce-scatter.2.cloned.1.call-update) | async-done | bytes 1048592 | tf_op jit(solution)/shard_map/reduce_scatter | solution.py:174
  414.1 2.5 copy.73
  416.6 4.6 all-to-all-start
  423.4 23.4 %all-to-all-done = f32[128,4,512]{0,2,1:T(8,128)S(1)} async-done(((f32[128,4,512]{0,2,1:T(8,128)}), f32[128,4,512]{0,2,1:T(8,128)S(1)}, u32[]{:S(2)}, u32[]{:S(2)}) %all-to-all-start) | async-done | bytes 1048608 | tf_op jit(solution)/shard_map/all_to_all | solution.py:175
  446.8 1.8 multiply_reduce_fusion.1
  450.5 2.2 fusion.118
  452.9 1.7 fusion.113
  454.6 31.0 %all-reduce.9.cloned.1.call-done = f32[512,64]{0,1:T(8,128)} async-done(((f32[512,64]{0,1:T(8,128)}), f32[512,64]{0,1:T(8,128)}) %all-reduce.9.cloned.1.call-update) | async-done | bytes 131088 | tf_op jit(solution)/shard_map/psum | solution.py:183
  485.6 1.3 copy.75
  486.9 18.4 %all-reduce.5 = (f32[64,33]{0,1:T(8,128)S(1)}, f32[64]{0:T(128)S(1)}, f32[64,64]{1,0:T(8,128)S(1)}, f32[2,64]{1,0:T(2,128)S(1)}, f32[512]{0:T(512)S(1)}) all-reduce(f32[64,33]{0,1:T(8,128)S(1)} %fusion.129, f32[64]{0:T(128)S(1)} %get-tuple-element.198, f32[64,64]{1,0:T(8,128)S(1)} %fusion.131, ...), channel_id=1, replica_groups=mesh['dp'=8,'chan'=4] {'chan'}, use_global_device_ids=true, to_apply=%region_3.4 | all-reduce | flops 6912 | bytes 55296 | tf_op jit(solution)/shard_map/psum | solution.py:183
  505.4 23.4 %all-reduce.4 = (f32[64,33]{0,1:T(8,128)}, f32[64]{0:T(128)}, f32[64,64]{1,0:T(8,128)}, f32[2,64]{1,0:T(2,128)}, f32[512]{0:T(512)}) all-reduce(f32[64,33]{0,1:T(8,128)S(1)} %get-tuple-element.214, f32[64]{0:T(128)S(1)} %get-tuple-element.215, f32[64,64]{1,0:T(8,128)S(1)} %get-tuple-element.216, ...), channel_id=1, replica_groups=mesh['dp'=8,'chan'=4] {'dp'}, use_global_device_ids=true, to_apply=%region_4.5 | all-reduce | flops 6912 | bytes 55296 | tf_op jit(solution)/shard_map/psum | solution.py:182
  528.8 13.0 %all-reduce.11.cloned.1.call-done = f32[512,64]{0,1:T(8,128)} async-done(((f32[512,64]{0,1:T(8,128)}), f32[512,64]{0,1:T(8,128)}) %all-reduce.11.cloned.1.call-update) | async-done | bytes 131088 | tf_op jit(solution)/shard_map/psum | solution.py:182
  541.8 1.6 copy.125
  (593 shorter events, 275.7 us)
Async XLA Ops:
  7.2 439.6 %copy-start = (f32[512,64]{0,1:T(8,128)S(1)}, f32[512,64]{0,1:T(8,128)}, u32[]{:S(2)}) copy-start(f32[512,64]{0,1:T(8,128)} %param.16) | copy-start | bytes 393220
  7.2 406.9 %reduce-scatter.2.cloned.1.call-start = ((), (), s32[]{:S(2)}) async-start(), calls=%async_computation.2 | async-start | bytes 9437184 | tf_op jit(solution)/shard_map/reduce_scatter | solution.py:174
  339.7 0.7 copy-start.3
  339.7 82.6 %copy-start.4 = (f32[2,64]{1,0:T(2,128)S(1)}, f32[2,64]{1,0:T(2,128)}, u32[]{:S(2)}) copy-start(f32[2,64]{1,0:T(2,128)} %param.15) | copy-start | bytes 1540
  339.7 82.6 %copy-start.2 = (f32[64,33]{0,1:T(8,128)S(1)}, f32[64,33]{0,1:T(8,128)}, u32[]{:S(2)}) copy-start(f32[64,33]{0,1:T(8,128)} %param.12) | copy-start | bytes 25348
  339.7 82.6 %copy-start.5 = (f32[64]{0:T(128)S(1)}, f32[64]{0:T(128)}, u32[]{:S(2)}) copy-start(f32[64]{0:T(128)} %param.13) | copy-start | bytes 772
  339.7 82.9 %copy-start.1 = (f32[64,64]{1,0:T(8,128)S(1)}, f32[64,64]{1,0:T(8,128)}, u32[]{:S(2)}) copy-start(f32[64,64]{1,0:T(8,128)} %param.14) | copy-start | bytes 49156
  416.6 30.2 %all-to-all-start = ((f32[128,4,512]{0,2,1:T(8,128)}), f32[128,4,512]{0,2,1:T(8,128)S(1)}, u32[]{:S(2)}, u32[]{:S(2)}) async-start(f32[128,4,512]{0,2,1:T(8,128)} %bitcast.39), calls=%async_computation.1 | async-start | bytes 2097152 | tf_op jit(solution)/shard_map/all_to_all | solution.py:175
  421.2 64.4 %all-reduce.9.cloned.1.call-start = ((), (), s32[]{:S(2)}) async-start(), calls=%async_computation.3 | async-start | bytes 262144 | tf_op jit(solution)/shard_map/psum | solution.py:183
  452.7 89.1 %all-reduce.11.cloned.1.call-start = ((), (), s32[]{:S(2)}) async-start(), calls=%async_computation.4 | async-start | bytes 262144 | tf_op jit(solution)/shard_map/psum | solution.py:182
Sparse Core Ops, SparseCore 0:
  339.8 74.2 reduce-scatter.1
  452.8 32.7 all-reduce.8
  488.6 53.0 all-reduce.10
